TPU v7x, 256 devices: a whole 4x4x8 slice. The times are simulated.
256 devices in a mesh: gx: 64 (over z, x, core), gy: 4 (over y).
Axes of the slice: x: 4, y: 4, z: 8, core: 2. Of those that a mesh axis runs over, the one named last changes fastest.
Arguments:
- adjoint_block: float32 [4, 3, 64, 256, 512], P(None, None, None, 'gx', 'gy'), may hold values from -18 to 18
- base_flow: float32 [2, 3, 64, 256, 512], P(None, None, None, 'gx', 'gy'), may hold values from -4 to 4
- direct_modes: float32 [8, 3, 64, 256, 512], P(None, None, None, 'gx', 'gy'), may hold values from -0.0012207031 to 0.0012207031
- dual_modes: float32 [8, 3, 64, 256, 512], P(None, None, None, 'gx', 'gy'), may hold values from -0.6 to 0.6
Outputs:
- next_block: float32 [4, 3, 64, 256, 512], P(None, None, None, 'gx', 'gy')
- growth: float32 [4, 4], replicated
All inputs are finite; a program needn't handle non-finite values.
Results may differ from a plain program's by a relative error of at most 0.0001.
Values sent between devices are 32-bit elements; how exact they have to be, the bound alone decides.
A program may use at most 128 MiB of HBM per device.

v0:
```python
import math
import jax
import jax.numpy as jnp
from jax import lax
from jax.sharding import PartitionSpec as P

step_size = 0.1
viscosity = 0.2


def padded_2(shard, sides, width):
    for axis, dim in sides:
        count, length = (lax.axis_size(axis), shard.shape[dim])
        up = [(i, (i + 1) % count) for i in range(count - 1)]
        down = [(j, i) for i, j in up]
        last = lax.slice_in_dim(shard, length - width, length, axis=dim)
        leading = lax.slice_in_dim(shard, 0, width, axis=dim)
        before = lax.ppermute(last, axis, up)
        after = lax.ppermute(leading, axis, down)
        shard = jnp.concatenate([before, shard, after], axis=dim)
    return shard


def central_x(padded):
    return 0.5 * (padded[..., 2:, 1:-1] - padded[..., :-2, 1:-1])


def central_y(padded):
    return 0.5 * (padded[..., 1:-1, 2:] - padded[..., 1:-1, :-2])


def central_z(interior):
    return 0.5 * (jnp.roll(interior, -1, axis=-3) - jnp.roll(interior, 1, axis=-3))


def laplace(padded):
    interior = padded[..., 1:-1, 1:-1]
    beside_all = (
        padded[..., 2:, 1:-1]
        + padded[..., :-2, 1:-1]
        + padded[..., 1:-1, 2:]
        + padded[..., 1:-1, :-2]
    )
    beside_all = beside_all + jnp.roll(interior, -1, axis=-3) + jnp.roll(interior, 1, axis=-3)
    return beside_all - 6.0 * interior


def base_terms(padded_base):
    centre = padded_base[..., 1:-1, 1:-1]
    gradients = jnp.stack([central_x(padded_base), central_y(padded_base), central_z(centre)])
    return (centre, gradients)


def adjoint_step(padded, centre, gradients):
    interior = padded[..., 1:-1, 1:-1]
    advect = (
        centre[0] * central_x(padded)
        + centre[1] * central_y(padded)
        + centre[2] * central_z(interior)
    )
    produce = jnp.sum(interior[:, None] * gradients[None], axis=2)
    return interior + step_size * (advect - produce + viscosity * laplace(padded))


def project(left, right):
    return lax.dot_general(
        left,
        right,
        (((1,), (1,)), ((), ())),
        precision=lax.Precision.HIGHEST,
        preferred_element_type=jnp.float32,
    )


def combine_modes(coefficients, modes):
    return jnp.dot(
        coefficients.T, modes, precision=lax.Precision.HIGHEST, preferred_element_type=jnp.float32
    )


def extend_vectors(field):
    vectors, comps, depth, width_x, width_y = field.shape
    merged = field.reshape(vectors * comps, depth, width_x, width_y)
    padded = padded_2(merged, (("gx", 2), ("gy", 3)), 1)
    return padded.reshape(vectors, comps, depth, width_x + 2, width_y + 2)


def body(adjoint_block, base_flow, direct_modes, dual_modes):
    vectors, comps, depth, width_x, width_y = adjoint_block.shape
    mode_count = direct_modes.shape[0]
    row_count = comps * depth * width_x * width_y
    cell_total = float(
        comps * depth * width_x * lax.axis_size("gx") * width_y * lax.axis_size("gy")
    )
    padded_base = padded_2(
        base_flow.reshape(2 * comps, depth, width_x, width_y), (("gx", 2), ("gy", 3)), 1
    )
    padded_base = padded_base.reshape(2, comps, depth, width_x + 2, width_y + 2)
    direct_flat = direct_modes.reshape(mode_count, row_count)
    dual_flat = dual_modes.reshape(mode_count, row_count)
    padded = extend_vectors(adjoint_block)
    for substep in range(2):
        centre, gradients = base_terms(padded_base[substep])
        advanced = adjoint_step(padded, centre, gradients)
        flattened = advanced.reshape(vectors, row_count)
        partial_terms = project(direct_flat, flattened)
        coefficients = lax.psum(partial_terms, ("gx", "gy"))
        deflated = flattened - combine_modes(coefficients, dual_flat)
        if substep == 0:
            padded = extend_vectors(deflated.reshape(advanced.shape))
    gram_matrix = lax.psum(project(deflated, deflated), ("gx", "gy"))
    cholesky_factor = jnp.linalg.cholesky(gram_matrix)
    solved = jax.scipy.linalg.solve_triangular(cholesky_factor, deflated, lower=True)
    next_block = (math.sqrt(cell_total) * solved).reshape(adjoint_block.shape)
    return (next_block, cholesky_factor)


def solution(mesh):
    placed = (
        P(None, None, None, "gx", "gy"),
        P(None, None, None, "gx", "gy"),
        P(None, None, None, "gx", "gy"),
        P(None, None, None, "gx", "gy"),
    )
    return jax.shard_map(
        body,
        mesh=mesh,
        in_specs=placed,
        out_specs=(P(None, None, None, "gx", "gy"), P()),
        check_vma=False,
    )
```

profile of v0, /device:TPU:1, one launch (start us, length us, event | category | flops | bytes accessed | tf_op | source)
XLA Modules:
  0.0 437.2 jit_solution(15457875989147088941)
XLA Ops:
  0.6 2.9 copy.146
  3.5 2.2 fusion.43
  5.7 5.1 %collective-permute-start.4 = (f32[6,64,1,128]{1,3,2,0:T(8,128)}, f32[6,64,1,128]{1,3,2,0:T(8,128)S(1)}, u32[]{:S(2)}, u32[]{:S(2)}) collective-permute-start(f32[6,64,1,128]{1,3,2,0:T(8,128)} %get-tuple-element.41), channel_id=1, source_target_pairs={{4,0},{8,4},{12,8},{16,12},{20,16},{24,20},{28,24},{32,28},{36,32}... | collective-permute-start | bytes 589832 | tf_op jit(solution)/shard_map/ppermute | solution.py:19
  10.9 1.9 collective-permute-start.5
  13.0 1.2 copy-done.5
  15.2 3.1 collective-permute-start.1
  18.3 2.4 collective-permute-start
  20.7 2.3 slice_bitcast_fusion.5
  23.0 2.1 slice_bitcast_fusion.4
  25.1 1.2 fusion.30
  26.3 1.7 copy.149
  28.0 1.7 copy.148
  29.7 1.7 copy.147
  31.4 5.1 %reshape.186 = f32[8,98304]{1,0:T(8,128)} reshape(f32[8,3,64,4,128]{4,3,2,1,0:T(4,128)} %param.7) | data formatting | bytes 6291456 | tf_op jit(solution)/shard_map/reshape | solution.py:100
  36.5 4.9 %fusion.26 = (f32[1,3,64,4,128]{2,4,3,1,0:T(8,128)}, f32[1,3,64,4,128]{2,4,3,1,0:T(8,128)}) fusion(f32[1,3,1,4,128]{2,4,3,1,0:T(8,128)} %get-tuple-element.35, f32[1,3,63,4,128]{2,4,3,1,0:T(8,128)} %get-tuple-element.39, f32[1,3,63,4,128]{2,4,3,1,0:T(8,128)} %get-tuple-element.36, f32[1,3,1,4,128]{2,4,3,1,0:T(8,128)} %get-tuple-element.32, ...), kind=kLoop, calls=%fused_computation.53 | loop fusion | flops 786432 | bytes 2359296 | tf_op jit(solution)/shard_map/mul | solution.py:33
  42.3 2.6 collective-permute-start.7
  44.8 1.3 collective-permute-start.6
  46.1 2.4 fusion.25
  49.3 1.5 fusion.23
  50.9 1.3 pad_maximum_fusion.2
  52.2 3.1 fusion.40
  55.4 2.4 copy.143
  57.8 1.3 collective-permute-start.3
  59.1 2.4 copy.142
  61.5 4.5 %collective-permute-start.2 = (f32[12,64,6,1]{1,3,2,0:T(1,128)S(1)}, f32[12,64,6,1]{1,3,2,0:T(1,128)S(1)}, u32[]{:S(2)}, u32[]{:S(2)}) collective-permute-start(f32[12,64,6,1]{1,3,2,0:T(1,128)S(1)} %copy.142), channel_id=1, source_target_pairs={{0,1},{1,2},{2,3},{4,5},{5,6},{6,7},{8,9},{9,10},{10,11},{12,13},{... | collective-permute-start | bytes 55304 | tf_op jit(solution)/shard_map/ppermute | solution.py:18
  66.0 3.3 pad_maximum_fusion.3
  69.3 2.8 copy.152
  72.2 2.2 copy.145
  74.4 2.2 copy.144
  76.6 4.9 %pad_maximum_fusion.1 = f32[12,64,6,130]{3,1,2,0:T(8,128)S(1)} fusion(f32[12,64,6,1]{3,1,2,0:T(8,128)} %copy.145, f32[12,64,1,128]{3,1,2,0:T(8,128)} %collective-permute-done.1, f32[12,64,4,128]{3,1,2,0:T(8,128)} %bitcast.87, f32[12,64,1,128]{3,1,2,0:T(8,128)} %collective-permute-done, f32[12,64,6,1]{3,1,2,0:T(8,128)} %copy.144), kind=kLoop, calls=%fused_computation.4 | loop fusion | flops 2396160 | bytes 4792320 | tf_op jit(solution)/shard_map/concatenate | solution.py:20
  84.2 2.1 multiply_add_fusion.1
  86.3 2.2 copy.153
  88.5 8.9 %fusion.6 = f32[8,4]{0,1:T(4,128)S(1)} fusion(f32[8,3,64,4,128]{4,3,2,1,0:T(4,128)S(1)} %copy-done, f32[4,3,64,4,128]{4,2,3,1,0:T(8,128)S(1)} %multiply_add_fusion.1), kind=kOutput, calls=%fused_computation.22 | convolution fusion | flops 37748736 | bytes 4718720 | tf_op jit(solution)/shard_map/dot_general | solution.py:66
  97.4 3.6 reshape.185
  101.1 83.8 %psum.21 = f32[8,4]{0,1:T(4,128)S(1)} all-reduce(f32[8,4]{0,1:T(4,128)S(1)} %fusion.6), channel_id=1, replica_groups=mesh['gx'=64,'gy'=4] {'gx','gy'}, use_global_device_ids=true, to_apply=%region_1.2 | all-reduce | flops 32 | bytes 256 | tf_op jit(solution)/shard_map/psum | solution.py:107
  184.9 6.2 %convolution_subtract_fusion.1 = f32[4,98304]{1,0:T(4,128)} fusion(f32[4,98304]{1,0:T(4,128)} %reshape.185, f32[8,4]{0,1:T(4,128)S(1)} %psum.21, f32[8,98304]{1,0:T(8,128)} %reshape.186), kind=kOutput, calls=%fused_computation.2 | convolution fusion | flops 38141952 | bytes 6291584 | tf_op jit(solution)/shard_map/dot_general | solution.py:76
  191.1 3.9 reshape_reshape.3
  195.0 3.6 fusion.41
  198.7 2.6 collective-permute-start.9
  201.3 3.0 collective-permute-start.8
  205.3 1.7 copy.163
  207.8 3.3 copy.159
  211.1 2.2 copy.160
  213.3 2.2 copy.158
  215.5 1.3 pad_maximum_fusion.19
  216.8 1.3 collective-permute-start.11
  218.1 4.0 collective-permute-start.10
  222.1 1.6 pad_maximum_fusion.4
  223.7 2.8 copy.167
  226.6 4.3 pad_maximum_fusion
  230.8 6.3 %copy.161 = f32[12,64,6,130]{3,1,2,0:T(8,128)} copy(f32[12,64,6,130]{1,3,2,0:T(8,128)} %pad_maximum_fusion) | data formatting | bytes 4792320 | tf_op jit(solution)/shard_map/concatenate | solution.py:20
  237.2 2.4 slice.360
  239.5 3.9 fusion.36
  245.0 2.3 multiply_add_fusion
  247.4 2.2 copy.168
  249.5 8.9 %fusion.11 = f32[8,4]{0,1:T(4,128)S(1)} fusion(f32[8,3,64,4,128]{4,3,2,1,0:T(4,128)S(1)} %copy-done, f32[4,3,64,4,128]{4,2,3,1,0:T(8,128)S(1)} %multiply_add_fusion), kind=kOutput, calls=%fused_computation.23 | convolution fusion | flops 37748736 | bytes 4718720 | tf_op jit(solution)/shard_map/dot_general | solution.py:66
  258.5 3.6 reshape.188
  262.1 75.8 %psum.22 = f32[8,4]{0,1:T(4,128)S(1)} all-reduce(f32[8,4]{0,1:T(4,128)S(1)} %fusion.11), channel_id=1, replica_groups=mesh['gx'=64,'gy'=4] {'gx','gy'}, use_global_device_ids=true, to_apply=%region_3.4 | all-reduce | flops 32 | bytes 256 | tf_op jit(solution)/shard_map/psum | solution.py:107
  337.9 5.1 %convolution_subtract_fusion = f32[4,98304]{1,0:T(4,128)S(1)} fusion(f32[4,98304]{1,0:T(4,128)} %reshape.188, f32[8,4]{0,1:T(4,128)S(1)} %psum.22, f32[8,98304]{1,0:T(8,128)} %reshape.186), kind=kOutput, calls=%fused_computation.1 | convolution fusion | flops 38141952 | bytes 6291584 | tf_op jit(solution)/shard_map/dot_general | solution.py:76
  344.2 6.8 %fusion.44 = f32[4,4]{0,1:T(4,128)S(1)} fusion(f32[4,98304]{1,0:T(4,128)S(1)} %convolution_subtract_fusion), kind=kOutput, calls=%fused_computation.91 | convolution fusion | flops 18874368 | bytes 1572928 | tf_op jit(solution)/shard_map/dot_general | solution.py:66
  351.0 73.8 %psum.23 = f32[4,4]{0,1:T(4,128)S(1)} all-reduce(f32[4,4]{0,1:T(4,128)S(1)} %fusion.44), channel_id=1, replica_groups=mesh['gx'=64,'gy'=4] {'gx','gy'}, use_global_device_ids=true, to_apply=%region_4.5 | all-reduce | flops 16 | bytes 128 | tf_op jit(solution)/shard_map/psum | solution.py:111
  426.0 1.3 select_bitcast_fusion
  427.6 5.5 %convolution_multiply_fusion = f32[4,98304]{1,0:T(4,128)} fusion(f32[4,98304]{1,0:T(4,128)} %copy-done.4, f32[1,4,4]{1,2,0:T(4,128)S(1)} %custom-call.7), kind=kOutput, calls=%fused_computation | convolution fusion | flops 19267584 | bytes 3145792 | tf_op jit(solution)/shard_map/jit(_solve_triangular)/triangular_solve | solution.py:113
  433.1 3.9 reshape.189
  (66 shorter events, 11.7 us)
Async XLA Ops:
  0.6 87.9 %copy-start = (f32[8,3,64,4,128]{4,3,2,1,0:T(4,128)S(1)}, f32[8,3,64,4,128]{4,3,2,1,0:T(4,128)}, u32[]{:S(2)}) copy-start(f32[8,3,64,4,128]{4,3,2,1,0:T(4,128)} %param.6) | copy-start | bytes 9437188
  3.5 9.2 %copy-start.12 = (f32[4,3,64,4,128]{4,3,2,1,0:T(4,128)S(1)}, f32[4,3,64,4,128]{4,3,2,1,0:T(4,128)}, u32[]{:S(2)}) copy-start(f32[4,3,64,4,128]{4,3,2,1,0:T(4,128)} %param.4) | copy-start | bytes 4718596
  5.7 35.7 %collective-permute-start.4 = (f32[6,64,1,128]{1,3,2,0:T(8,128)}, f32[6,64,1,128]{1,3,2,0:T(8,128)S(1)}, u32[]{:S(2)}, u32[]{:S(2)}) collective-permute-start(f32[6,64,1,128]{1,3,2,0:T(8,128)} %get-tuple-element.41), channel_id=1, source_target_pairs={{4,0},{8,4},{12,8},{16,12},{20,16},{24,20},{28,24},{32,28},{36,32}... | collective-permute-start | bytes 589832 | tf_op jit(solution)/shard_map/ppermute | solution.py:19
  10.9 30.6 %collective-permute-start.5 = (f32[6,64,1,128]{1,3,2,0:T(8,128)}, f32[6,64,1,128]{1,3,2,0:T(8,128)}, u32[]{:S(2)}, u32[]{:S(2)}) collective-permute-start(f32[6,64,1,128]{1,3,2,0:T(8,128)} %get-tuple-element.40), channel_id=1, source_target_pairs={{0,4},{4,8},{8,12},{12,16},{16,20},{20,24},{24,28},{28,32},{32,36}... | collective-permute-start | bytes 589832 | tf_op jit(solution)/shard_map/ppermute | solution.py:18
  13.0 1.2 copy-start.5
  13.0 7.7 %copy-start.1 = (f32[2,3,64,4,128]{2,4,3,1,0:T(8,128)S(1)}, f32[2,3,64,4,128]{2,4,3,1,0:T(8,128)}, u32[]{:S(2)}) copy-start(f32[2,3,64,4,128]{2,4,3,1,0:T(8,128)} %copy.146) | copy-start | bytes 2359300
  15.2 35.7 %collective-permute-start.1 = (f32[12,64,1,128]{3,1,2,0:T(8,128)}, f32[12,64,1,128]{3,1,2,0:T(8,128)}, u32[]{:S(2)}, u32[]{:S(2)}) collective-permute-start(f32[12,64,1,128]{3,1,2,0:T(8,128)} %get-tuple-element.31), channel_id=1, source_target_pairs={{4,0},{8,4},{12,8},{16,12},{20,16},{24,20},{28,24},{32,28},{36,32}... | collective-permute-start | bytes 1179656 | tf_op jit(solution)/shard_map/ppermute | solution.py:19
  18.3 32.6 %collective-permute-start = (f32[12,64,1,128]{3,1,2,0:T(8,128)}, f32[12,64,1,128]{3,1,2,0:T(8,128)}, u32[]{:S(2)}, u32[]{:S(2)}) collective-permute-start(f32[12,64,1,128]{3,1,2,0:T(8,128)} %get-tuple-element.30), channel_id=1, source_target_pairs={{0,4},{4,8},{8,12},{12,16},{16,20},{20,24},{24,28},{28,32},{32,36}... | collective-permute-start | bytes 1179656 | tf_op jit(solution)/shard_map/ppermute | solution.py:18
  36.5 4.9 %copy-start.2 = (f32[2,3,64,4,128]{2,4,3,1,0:T(8,128)S(1)}, f32[2,3,64,4,128]{2,4,3,1,0:T(8,128)}, u32[]{:S(2)}) copy-start(f32[2,3,64,4,128]{2,4,3,1,0:T(8,128)} %copy.146) | copy-start | bytes 2359300
  42.3 6.3 %collective-permute-start.7 = (f32[6,64,6,1]{1,3,2,0:T(1,128)S(1)}, f32[6,64,6,1]{1,3,2,0:T(1,128)S(1)}, u32[]{:S(2)}, u32[]{:S(2)}) collective-permute-start(f32[6,64,6,1]{1,3,2,0:T(1,128)S(1)} %get-tuple-element.21), channel_id=1, source_target_pairs={{0,1},{1,2},{2,3},{4,5},{5,6},{6,7},{8,9},{9,10},{10,11},{12,13},{... | collective-permute-start | bytes 27656 | tf_op jit(solution)/shard_map/ppermute | solution.py:18
  44.8 4.5 %collective-permute-start.6 = (f32[6,64,6,1]{1,3,2,0:T(1,128)S(1)}, f32[6,64,6,1]{1,3,2,0:T(1,128)S(1)}, u32[]{:S(2)}, u32[]{:S(2)}) collective-permute-start(f32[6,64,6,1]{1,3,2,0:T(1,128)S(1)} %get-tuple-element.20), channel_id=1, source_target_pairs={{1,0},{2,1},{3,2},{5,4},{6,5},{7,6},{9,8},{10,9},{11,10},{13,12},{... | collective-permute-start | bytes 27656 | tf_op jit(solution)/shard_map/ppermute | solution.py:19
  48.5 2.4 copy-start.6
  57.8 14.4 %collective-permute-start.3 = (f32[12,64,6,1]{1,3,2,0:T(1,128)S(1)}, f32[12,64,6,1]{1,3,2,0:T(1,128)S(1)}, u32[]{:S(2)}, u32[]{:S(2)}) collective-permute-start(f32[12,64,6,1]{1,3,2,0:T(1,128)S(1)} %copy.143), channel_id=1, source_target_pairs={{1,0},{2,1},{3,2},{5,4},{6,5},{7,6},{9,8},{10,9},{11,10},{13,12},{... | collective-permute-start | bytes 55304 | tf_op jit(solution)/shard_map/ppermute | solution.py:19
  61.5 12.9 %collective-permute-start.2 = (f32[12,64,6,1]{1,3,2,0:T(1,128)S(1)}, f32[12,64,6,1]{1,3,2,0:T(1,128)S(1)}, u32[]{:S(2)}, u32[]{:S(2)}) collective-permute-start(f32[12,64,6,1]{1,3,2,0:T(1,128)S(1)} %copy.142), channel_id=1, source_target_pairs={{0,1},{1,2},{2,3},{4,5},{5,6},{6,7},{8,9},{9,10},{10,11},{12,13},{... | collective-permute-start | bytes 55304 | tf_op jit(solution)/shard_map/ppermute | solution.py:18
  81.9 1.3 copy-start.7
  83.2 0.9 copy-start.14
  83.2 1.0 copy-start.15
  83.2 1.0 copy-start.16
  195.0 12.0 %copy-start.13 = (f32[64,4,128]{0,2,1:T(8,128)S(1)}, f32[64,4,128]{0,2,1:T(8,128)}, u32[]{:S(2)}) copy-start(f32[64,4,128]{0,2,1:T(8,128)} %get-tuple-element.22) | copy-start | bytes 393220
  198.7 12.4 %collective-permute-start.9 = (f32[12,64,1,128]{3,1,2,0:T(8,128)}, f32[12,64,1,128]{3,1,2,0:T(8,128)}, u32[]{:S(2)}, u32[]{:S(2)}) collective-permute-start(f32[12,64,1,128]{3,1,2,0:T(8,128)} %bitcast.36), channel_id=1, source_target_pairs={{4,0},{8,4},{12,8},{16,12},{20,16},{24,20},{28,24},{32,28},{36,32}... | collective-permute-start | bytes 1179656 | tf_op jit(solution)/shard_map/ppermute | solution.py:19
  201.3 12.1 %collective-permute-start.8 = (f32[12,64,1,128]{3,1,2,0:T(8,128)}, f32[12,64,1,128]{3,1,2,0:T(8,128)}, u32[]{:S(2)}, u32[]{:S(2)}) collective-permute-start(f32[12,64,1,128]{3,1,2,0:T(8,128)} %bitcast.35), channel_id=1, source_target_pairs={{0,4},{4,8},{8,12},{12,16},{16,20},{20,24},{24,28},{28,32},{32,36}... | collective-permute-start | bytes 1179656 | tf_op jit(solution)/shard_map/ppermute | solution.py:18
  215.5 6.6 %copy-start.9 = (f32[1,3,64,4,128]{2,4,3,1,0:T(8,128)S(1)}, f32[1,3,64,4,128]{2,4,3,1,0:T(8,128)}, u32[]{:S(2)}) copy-start(f32[1,3,64,4,128]{2,4,3,1,0:T(8,128)} %get-tuple-element.15) | copy-start | bytes 1179652
  215.5 6.6 %copy-start.10 = (f32[1,3,64,4,128]{2,4,3,1,0:T(8,128)S(1)}, f32[1,3,64,4,128]{2,4,3,1,0:T(8,128)}, u32[]{:S(2)}) copy-start(f32[1,3,64,4,128]{2,4,3,1,0:T(8,128)} %get-tuple-element.19) | copy-start | bytes 1179652
  215.5 6.6 %copy-start.11 = (f32[1,3,64,4,128]{2,4,3,1,0:T(8,128)S(1)}, f32[1,3,64,4,128]{2,4,3,1,0:T(8,128)}, u32[]{:S(2)}) copy-start(f32[1,3,64,4,128]{2,4,3,1,0:T(8,128)} %get-tuple-element.43) | copy-start | bytes 1179652
  216.8 9.8 %collective-permute-start.11 = (f32[12,64,6,1]{1,3,2,0:T(1,128)S(1)}, f32[12,64,6,1]{1,3,2,0:T(1,128)S(1)}, u32[]{:S(2)}, u32[]{:S(2)}) collective-permute-start(f32[12,64,6,1]{1,3,2,0:T(1,128)S(1)} %get-tuple-element.9), channel_id=1, source_target_pairs={{1,0},{2,1},{3,2},{5,4},{6,5},{7,6},{9,8},{10,9},{11,10},{13,12},{... | collective-permute-start | bytes 55304 | tf_op jit(solution)/shard_map/ppermute | solution.py:19
  218.1 8.5 %collective-permute-start.10 = (f32[12,64,6,1]{1,3,2,0:T(1,128)S(1)}, f32[12,64,6,1]{1,3,2,0:T(1,128)S(1)}, u32[]{:S(2)}, u32[]{:S(2)}) collective-permute-start(f32[12,64,6,1]{1,3,2,0:T(1,128)S(1)} %get-tuple-element.8), channel_id=1, source_target_pairs={{0,1},{1,2},{2,3},{4,5},{5,6},{6,7},{8,9},{9,10},{10,11},{12,13},{... | collective-permute-start | bytes 55304 | tf_op jit(solution)/shard_map/ppermute | solution.py:18
  239.5 4.2 copy-start.3
  239.5 4.5 %copy-start.8 = (f32[3,3,64,4,128]{4,2,3,1,0:T(8,128)S(1)}, f32[3,3,64,4,128]{4,2,3,1,0:T(8,128)}, u32[]{:S(2)}) copy-start(f32[3,3,64,4,128]{4,2,3,1,0:T(8,128)} %copy.167) | copy-start | bytes 3538948
  244.1 0.9 copy-start.17
  244.1 1.0 copy-start.18
  343.0 1.1 copy-start.4
where the time goes:
time: 444 us; the launch traced here: 437 us
  blocking collectives  233 us (52%)
  local copies, waits for them, and re-layouts  91.6 us (21%)
  matrix products  41.5 us (9%)
  other arithmetic  35.5 us (8%)
  starting transfers between devices  33.1 us (7%)
    psum x2, blocking collectives, body(): coefficients = lax.psum(partial_terms, ('gx', 'gy'))  160 us
    psum x1, blocking collectives, body(): gram_matrix = lax.psum(project(deflated, deflated), ('gx', 'gy'))  73.8 us
    dot_general x3, matrix products, project(): lax.dot_general(left, right, (((1,), (1,)), ((), ())), precision=lax.Prec...  24.7 us
    ppermute x6, starting transfers between devices, padded_2(): before = lax.ppermute(last, axis, up)  18.4 us
    ppermute x6, starting transfers between devices, padded_2(): after = lax.ppermute(leading, axis, down)  14.7 us
    slice x5, local copies, waits for them, and re-layouts, padded_2(): last = lax.slice_in_dim(shard, length - width, length, axis=dim)  12.3 us
    dot_general x2, matrix products, combine_modes(): jnp.dot(coefficients.T, modes, precision=lax.Precision.HIGHEST, preferred...  11.3 us
    concatenate x3, other arithmetic, padded_2(): shard = jnp.concatenate([before, shard, after], axis=dim)  10.5 us
  transfers between devices with their start and end apart: 12, of which 1 were waited for; matrix products, arithmetic and copies ran while one was open for 12% of the time, Pallas kernels for 0%

commit v1 on v0

--- a/solution.py
+++ b/solution.py
@@ -108,7 +108,9 @@
         deflated = flattened - combine_modes(coefficients, dual_flat)
         if substep == 0:
             padded = extend_vectors(deflated.reshape(advanced.shape))
-    gram_matrix = lax.psum(project(deflated, deflated), ("gx", "gy"))
+    gram_matrix = project(deflated, deflated)
+    for mesh_axis in ("gy", "gx"):
+        gram_matrix = lax.psum(gram_matrix, mesh_axis)
     cholesky_factor = jnp.linalg.cholesky(gram_matrix)
     solved = jax.scipy.linalg.solve_triangular(cholesky_factor, deflated, lower=True)
     next_block = (math.sqrt(cell_total) * solved).reshape(adjoint_block.shape)

time: 444 us -> 505 us (1.14)
  blocking collectives: 233 us -> 294 us
    psum x1 -> x2, blocking collectives: 73.8 us -> 134 us  [body(): gram_matrix = lax.psum(gram_matrix, mesh_axis)]
  transfers between devices with their start and end apart: 12 -> 12, of which waited for: 1 -> 1; matrix products, arithmetic and copies ran while one was open for 12% -> 10% of each run, Pallas kernels for 0% -> 0%
where the time goes in v1:
time: 505 us; the launch traced here: 498 us
  blocking collectives  294 us (58%)
  local copies, waits for them, and re-layouts  91.5 us (18%)
  matrix products  41.5 us (8%)
  other arithmetic  35.4 us (7%)
  starting transfers between devices  33.1 us (7%)
    psum x2, blocking collectives, body(): coefficients = lax.psum(partial_terms, ('gx', 'gy'))  160 us
    psum x2, blocking collectives, body(): gram_matrix = lax.psum(gram_matrix, mesh_axis)  134 us
    dot_general x3, matrix products, project(): lax.dot_general(left, right, (((1,), (1,)), ((), ())), precision=lax.Prec...  24.7 us
    ppermute x6, starting transfers between devices, padded_2(): before = lax.ppermute(last, axis, up)  18.4 us
    ppermute x6, starting transfers between devices, padded_2(): after = lax.ppermute(leading, axis, down)  14.7 us
    slice x5, local copies, waits for them, and re-layouts, padded_2(): last = lax.slice_in_dim(shard, length - width, length, axis=dim)  12.3 us
    dot_general x2, matrix products, combine_modes(): jnp.dot(coefficients.T, modes, precision=lax.Precision.HIGHEST, preferred...  11.3 us
    concatenate x3, other arithmetic, padded_2(): shard = jnp.concatenate([before, shard, after], axis=dim)  10.5 us
  transfers between devices with their start and end apart: 12, of which 1 were waited for; matrix products, arithmetic and copies ran while one was open for 10% of the time, Pallas kernels for 0%

profile of v1, /device:TPU:1, one launch (start us, length us, event | category | flops | bytes accessed | tf_op | source)
XLA Modules:
  0.0 497.6 jit_solution(13332402243412527005)
XLA Ops:
  0.6 2.9 copy.146
  3.5 2.2 fusion.43
  5.7 5.1 %collective-permute-start.4 = (f32[6,64,1,128]{1,3,2,0:T(8,128)}, f32[6,64,1,128]{1,3,2,0:T(8,128)S(1)}, u32[]{:S(2)}, u32[]{:S(2)}) collective-permute-start(f32[6,64,1,128]{1,3,2,0:T(8,128)} %get-tuple-element.41), channel_id=1, source_target_pairs={{4,0},{8,4},{12,8},{16,12},{20,16},{24,20},{28,24},{32,28},{36,32}... | collective-permute-start | bytes 589832 | tf_op jit(solution)/shard_map/ppermute | solution.py:19
  10.9 1.9 collective-permute-start.5
  13.1 1.2 copy-done.5
  15.2 3.1 collective-permute-start.1
  18.3 2.4 collective-permute-start
  20.7 2.2 slice_bitcast_fusion.5
  23.0 2.1 slice_bitcast_fusion.4
  26.2 1.7 copy.149
  27.9 1.7 copy.148
  29.7 1.7 copy.147
  31.4 5.1 %reshape.186 = f32[8,98304]{1,0:T(8,128)} reshape(f32[8,3,64,4,128]{4,3,2,1,0:T(4,128)} %param.7) | data formatting | bytes 6291456 | tf_op jit(solution)/shard_map/reshape | solution.py:100
  36.5 4.9 fusion.26
  42.2 2.6 collective-permute-start.7
  44.8 1.3 collective-permute-start.6
  46.1 2.4 fusion.25
  49.3 1.5 fusion.23
  50.9 1.3 pad_maximum_fusion.2
  52.2 3.1 fusion.40
  55.3 2.4 copy.143
  57.7 1.3 collective-permute-start.3
  59.0 2.4 copy.142
  61.5 4.5 collective-permute-start.2
  66.0 3.3 pad_maximum_fusion.3
  69.3 2.8 copy.152
  72.1 2.2 copy.145
  74.3 2.2 copy.144
  76.5 4.9 pad_maximum_fusion.1
  84.2 2.1 multiply_add_fusion.1
  86.3 2.2 copy.153
  88.4 8.9 %fusion.6 = f32[8,4]{0,1:T(4,128)S(1)} fusion(f32[8,3,64,4,128]{4,3,2,1,0:T(4,128)S(1)} %copy-done, f32[4,3,64,4,128]{4,2,3,1,0:T(8,128)S(1)} %multiply_add_fusion.1), kind=kOutput, calls=%fused_computation.22 | convolution fusion | flops 37748736 | bytes 4718720 | tf_op jit(solution)/shard_map/dot_general | solution.py:66
  97.4 3.6 reshape.185
  101.0 83.8 %psum.28 = f32[8,4]{0,1:T(4,128)S(1)} all-reduce(f32[8,4]{0,1:T(4,128)S(1)} %fusion.6), channel_id=1, replica_groups=mesh['gx'=64,'gy'=4] {'gx','gy'}, use_global_device_ids=true, to_apply=%region_1.2 | all-reduce | flops 32 | bytes 256 | tf_op jit(solution)/shard_map/psum | solution.py:107
  184.8 6.2 %convolution_subtract_fusion.1 = f32[4,98304]{1,0:T(4,128)} fusion(f32[4,98304]{1,0:T(4,128)} %reshape.185, f32[8,4]{0,1:T(4,128)S(1)} %psum.28, f32[8,98304]{1,0:T(8,128)} %reshape.186), kind=kOutput, calls=%fused_computation.2 | convolution fusion | flops 38141952 | bytes 6291584 | tf_op jit(solution)/shard_map/dot_general | solution.py:76
  191.0 3.9 reshape_reshape.3
  194.9 3.6 fusion.41
  198.6 2.6 collective-permute-start.9
  201.1 3.0 collective-permute-start.8
  205.2 1.7 copy.163
  207.7 3.3 copy.159
  211.0 2.2 copy.160
  213.2 2.2 copy.158
  215.3 1.3 pad_maximum_fusion.19
  216.6 1.3 collective-permute-start.11
  217.9 4.0 collective-permute-start.10
  222.0 1.6 pad_maximum_fusion.4
  223.6 2.8 copy.167
  226.4 4.3 pad_maximum_fusion
  230.7 6.3 %copy.161 = f32[12,64,6,130]{3,1,2,0:T(8,128)} copy(f32[12,64,6,130]{1,3,2,0:T(8,128)} %pad_maximum_fusion) | data formatting | bytes 4792320 | tf_op jit(solution)/shard_map/concatenate | solution.py:20
  237.0 2.4 slice.360
  239.4 3.9 fusion.36
  244.9 2.3 multiply_add_fusion
  247.2 2.2 copy.168
  249.4 8.9 %fusion.11 = f32[8,4]{0,1:T(4,128)S(1)} fusion(f32[8,3,64,4,128]{4,3,2,1,0:T(4,128)S(1)} %copy-done, f32[4,3,64,4,128]{4,2,3,1,0:T(8,128)S(1)} %multiply_add_fusion), kind=kOutput, calls=%fused_computation.23 | convolution fusion | flops 37748736 | bytes 4718720 | tf_op jit(solution)/shard_map/dot_general | solution.py:66
  258.3 3.6 reshape.188
  261.9 75.8 %psum.29 = f32[8,4]{0,1:T(4,128)S(1)} all-reduce(f32[8,4]{0,1:T(4,128)S(1)} %fusion.11), channel_id=1, replica_groups=mesh['gx'=64,'gy'=4] {'gx','gy'}, use_global_device_ids=true, to_apply=%region_3.4 | all-reduce | flops 32 | bytes 256 | tf_op jit(solution)/shard_map/psum | solution.py:107
  337.8 5.1 %convolution_subtract_fusion = f32[4,98304]{1,0:T(4,128)S(1)} fusion(f32[4,98304]{1,0:T(4,128)} %reshape.188, f32[8,4]{0,1:T(4,128)S(1)} %psum.29, f32[8,98304]{1,0:T(8,128)} %reshape.186), kind=kOutput, calls=%fused_computation.1 | convolution fusion | flops 38141952 | bytes 6291584 | tf_op jit(solution)/shard_map/dot_general | solution.py:76
  344.0 6.8 %fusion.44 = f32[4,4]{0,1:T(4,128)S(1)} fusion(f32[4,98304]{1,0:T(4,128)S(1)} %convolution_subtract_fusion), kind=kOutput, calls=%fused_computation.91 | convolution fusion | flops 18874368 | bytes 1572928 | tf_op jit(solution)/shard_map/dot_general | solution.py:66
  350.8 8.4 %psum.30 = f32[4,4]{0,1:T(4,128)S(1)} all-reduce(f32[4,4]{0,1:T(4,128)S(1)} %fusion.44), channel_id=1, replica_groups=mesh['gx'=64,'gy'=4] {'gy'}, use_global_device_ids=true, to_apply=%region_4.5 | all-reduce | flops 16 | bytes 128 | tf_op jit(solution)/shard_map/psum | solution.py:113
  359.2 126.1 %psum.31 = f32[4,4]{0,1:T(4,128)S(1)} all-reduce(f32[4,4]{0,1:T(4,128)S(1)} %psum.30), channel_id=1, replica_groups=mesh['gx'=64,'gy'=4] {'gx'}, use_global_device_ids=true, to_apply=%region_5.6 | all-reduce | flops 16 | bytes 128 | tf_op jit(solution)/shard_map/psum | solution.py:113
  486.4 1.2 select_bitcast_fusion
  488.0 5.5 %convolution_multiply_fusion = f32[4,98304]{1,0:T(4,128)} fusion(f32[4,98304]{1,0:T(4,128)} %copy-done.4, f32[1,4,4]{1,2,0:T(4,128)S(1)} %custom-call.7), kind=kOutput, calls=%fused_computation | convolution fusion | flops 19267584 | bytes 3145792 | tf_op jit(solution)/shard_map/jit(_solve_triangular)/triangular_solve | solution.py:115
  493.5 3.9 reshape.189
  (67 shorter events, 12.8 us)
Async XLA Ops:
  0.6 87.8 %copy-start = (f32[8,3,64,4,128]{4,3,2,1,0:T(4,128)S(1)}, f32[8,3,64,4,128]{4,3,2,1,0:T(4,128)}, u32[]{:S(2)}) copy-start(f32[8,3,64,4,128]{4,3,2,1,0:T(4,128)} %param.6) | copy-start | bytes 9437188
  3.5 9.3 %copy-start.12 = (f32[4,3,64,4,128]{4,3,2,1,0:T(4,128)S(1)}, f32[4,3,64,4,128]{4,3,2,1,0:T(4,128)}, u32[]{:S(2)}) copy-start(f32[4,3,64,4,128]{4,3,2,1,0:T(4,128)} %param.4) | copy-start | bytes 4718596
  5.7 35.7 %collective-permute-start.4 = (f32[6,64,1,128]{1,3,2,0:T(8,128)}, f32[6,64,1,128]{1,3,2,0:T(8,128)S(1)}, u32[]{:S(2)}, u32[]{:S(2)}) collective-permute-start(f32[6,64,1,128]{1,3,2,0:T(8,128)} %get-tuple-element.41), channel_id=1, source_target_pairs={{4,0},{8,4},{12,8},{16,12},{20,16},{24,20},{28,24},{32,28},{36,32}... | collective-permute-start | bytes 589832 | tf_op jit(solution)/shard_map/ppermute | solution.py:19
  10.9 30.5 %collective-permute-start.5 = (f32[6,64,1,128]{1,3,2,0:T(8,128)}, f32[6,64,1,128]{1,3,2,0:T(8,128)}, u32[]{:S(2)}, u32[]{:S(2)}) collective-permute-start(f32[6,64,1,128]{1,3,2,0:T(8,128)} %get-tuple-element.40), channel_id=1, source_target_pairs={{0,4},{4,8},{8,12},{12,16},{16,20},{20,24},{24,28},{28,32},{32,36}... | collective-permute-start | bytes 589832 | tf_op jit(solution)/shard_map/ppermute | solution.py:18
  13.0 1.2 copy-start.5
  13.1 7.7 %copy-start.1 = (f32[2,3,64,4,128]{2,4,3,1,0:T(8,128)S(1)}, f32[2,3,64,4,128]{2,4,3,1,0:T(8,128)}, u32[]{:S(2)}) copy-start(f32[2,3,64,4,128]{2,4,3,1,0:T(8,128)} %copy.146) | copy-start | bytes 2359300
  15.2 35.7 %collective-permute-start.1 = (f32[12,64,1,128]{3,1,2,0:T(8,128)}, f32[12,64,1,128]{3,1,2,0:T(8,128)}, u32[]{:S(2)}, u32[]{:S(2)}) collective-permute-start(f32[12,64,1,128]{3,1,2,0:T(8,128)} %get-tuple-element.31), channel_id=1, source_target_pairs={{4,0},{8,4},{12,8},{16,12},{20,16},{24,20},{28,24},{32,28},{36,32}... | collective-permute-start | bytes 1179656 | tf_op jit(solution)/shard_map/ppermute | solution.py:19
  18.3 32.6 %collective-permute-start = (f32[12,64,1,128]{3,1,2,0:T(8,128)}, f32[12,64,1,128]{3,1,2,0:T(8,128)}, u32[]{:S(2)}, u32[]{:S(2)}) collective-permute-start(f32[12,64,1,128]{3,1,2,0:T(8,128)} %get-tuple-element.30), channel_id=1, source_target_pairs={{0,4},{4,8},{8,12},{12,16},{16,20},{20,24},{24,28},{28,32},{32,36}... | collective-permute-start | bytes 1179656 | tf_op jit(solution)/shard_map/ppermute | solution.py:18
  36.5 5.0 copy-start.2
  42.2 6.3 %collective-permute-start.7 = (f32[6,64,6,1]{1,3,2,0:T(1,128)S(1)}, f32[6,64,6,1]{1,3,2,0:T(1,128)S(1)}, u32[]{:S(2)}, u32[]{:S(2)}) collective-permute-start(f32[6,64,6,1]{1,3,2,0:T(1,128)S(1)} %get-tuple-element.21), channel_id=1, source_target_pairs={{0,1},{1,2},{2,3},{4,5},{5,6},{6,7},{8,9},{9,10},{10,11},{12,13},{... | collective-permute-start | bytes 27656 | tf_op jit(solution)/shard_map/ppermute | solution.py:18
  44.8 4.5 collective-permute-start.6
  48.5 2.4 copy-start.6
  57.7 14.4 %collective-permute-start.3 = (f32[12,64,6,1]{1,3,2,0:T(1,128)S(1)}, f32[12,64,6,1]{1,3,2,0:T(1,128)S(1)}, u32[]{:S(2)}, u32[]{:S(2)}) collective-permute-start(f32[12,64,6,1]{1,3,2,0:T(1,128)S(1)} %copy.143), channel_id=1, source_target_pairs={{1,0},{2,1},{3,2},{5,4},{6,5},{7,6},{9,8},{10,9},{11,10},{13,12},{... | collective-permute-start | bytes 55304 | tf_op jit(solution)/shard_map/ppermute | solution.py:19
  61.5 12.9 %collective-permute-start.2 = (f32[12,64,6,1]{1,3,2,0:T(1,128)S(1)}, f32[12,64,6,1]{1,3,2,0:T(1,128)S(1)}, u32[]{:S(2)}, u32[]{:S(2)}) collective-permute-start(f32[12,64,6,1]{1,3,2,0:T(1,128)S(1)} %copy.142), channel_id=1, source_target_pairs={{0,1},{1,2},{2,3},{4,5},{5,6},{6,7},{8,9},{9,10},{10,11},{12,13},{... | collective-permute-start | bytes 55304 | tf_op jit(solution)/shard_map/ppermute | solution.py:18
  81.9 1.3 copy-start.7
  83.1 0.9 copy-start.14
  83.1 1.0 copy-start.15
  83.1 1.0 copy-start.16
  194.9 12.0 %copy-start.13 = (f32[64,4,128]{0,2,1:T(8,128)S(1)}, f32[64,4,128]{0,2,1:T(8,128)}, u32[]{:S(2)}) copy-start(f32[64,4,128]{0,2,1:T(8,128)} %get-tuple-element.22) | copy-start | bytes 393220
  198.6 12.4 %collective-permute-start.9 = (f32[12,64,1,128]{3,1,2,0:T(8,128)}, f32[12,64,1,128]{3,1,2,0:T(8,128)}, u32[]{:S(2)}, u32[]{:S(2)}) collective-permute-start(f32[12,64,1,128]{3,1,2,0:T(8,128)} %bitcast.36), channel_id=1, source_target_pairs={{4,0},{8,4},{12,8},{16,12},{20,16},{24,20},{28,24},{32,28},{36,32}... | collective-permute-start | bytes 1179656 | tf_op jit(solution)/shard_map/ppermute | solution.py:19
  201.1 12.0 %collective-permute-start.8 = (f32[12,64,1,128]{3,1,2,0:T(8,128)}, f32[12,64,1,128]{3,1,2,0:T(8,128)}, u32[]{:S(2)}, u32[]{:S(2)}) collective-permute-start(f32[12,64,1,128]{3,1,2,0:T(8,128)} %bitcast.35), channel_id=1, source_target_pairs={{0,4},{4,8},{8,12},{12,16},{16,20},{20,24},{24,28},{28,32},{32,36}... | collective-permute-start | bytes 1179656 | tf_op jit(solution)/shard_map/ppermute | solution.py:18
  215.3 6.6 %copy-start.9 = (f32[1,3,64,4,128]{2,4,3,1,0:T(8,128)S(1)}, f32[1,3,64,4,128]{2,4,3,1,0:T(8,128)}, u32[]{:S(2)}) copy-start(f32[1,3,64,4,128]{2,4,3,1,0:T(8,128)} %get-tuple-element.15) | copy-start | bytes 1179652
  215.3 6.6 %copy-start.10 = (f32[1,3,64,4,128]{2,4,3,1,0:T(8,128)S(1)}, f32[1,3,64,4,128]{2,4,3,1,0:T(8,128)}, u32[]{:S(2)}) copy-start(f32[1,3,64,4,128]{2,4,3,1,0:T(8,128)} %get-tuple-element.19) | copy-start | bytes 1179652
  215.3 6.6 %copy-start.11 = (f32[1,3,64,4,128]{2,4,3,1,0:T(8,128)S(1)}, f32[1,3,64,4,128]{2,4,3,1,0:T(8,128)}, u32[]{:S(2)}) copy-start(f32[1,3,64,4,128]{2,4,3,1,0:T(8,128)} %get-tuple-element.43) | copy-start | bytes 1179652
  216.6 9.8 %collective-permute-start.11 = (f32[12,64,6,1]{1,3,2,0:T(1,128)S(1)}, f32[12,64,6,1]{1,3,2,0:T(1,128)S(1)}, u32[]{:S(2)}, u32[]{:S(2)}) collective-permute-start(f32[12,64,6,1]{1,3,2,0:T(1,128)S(1)} %get-tuple-element.9), channel_id=1, source_target_pairs={{1,0},{2,1},{3,2},{5,4},{6,5},{7,6},{9,8},{10,9},{11,10},{13,12},{... | collective-permute-start | bytes 55304 | tf_op jit(solution)/shard_map/ppermute | solution.py:19
  217.9 8.5 %collective-permute-start.10 = (f32[12,64,6,1]{1,3,2,0:T(1,128)S(1)}, f32[12,64,6,1]{1,3,2,0:T(1,128)S(1)}, u32[]{:S(2)}, u32[]{:S(2)}) collective-permute-start(f32[12,64,6,1]{1,3,2,0:T(1,128)S(1)} %get-tuple-element.8), channel_id=1, source_target_pairs={{0,1},{1,2},{2,3},{4,5},{5,6},{6,7},{8,9},{9,10},{10,11},{12,13},{... | collective-permute-start | bytes 55304 | tf_op jit(solution)/shard_map/ppermute | solution.py:18
  239.4 4.2 copy-start.3
  239.4 4.5 copy-start.8
  243.9 0.9 copy-start.17
  243.9 1.0 copy-start.18
  342.9 1.1 copy-start.4
